TPU v7x, 32 devices: a whole 2x2x4 slice. The times are simulated.
32 devices in a mesh: scene: 2 (over y), bins: 4 (over z), az: 4 (over x, core).
Axes of the slice: x: 2, y: 2, z: 4, core: 2. Of those that a mesh axis runs over, the one named last changes fastest.
Arguments:
- raw_echoes: bfloat16 [2, 8, 512, 16384], P(None, ('scene', 'az'), 'bins'), parts along dimension 1, may hold values from -6 to 6
- range_phase: float32 [16384], replicated, may hold values from -3.140625 to 3.140625
- band_start: int32 [16384], replicated, may hold values from 0 to 16447, as said below
- band_weight: bfloat16 [8, 16384], replicated, may hold values from -0.25 to 0.75
- intersection_length: int32 [16384], P('bins'), may hold values from 32 to 128
- azimuth_rate: float32 [16384], P('bins'), may hold values from 0.25 to 2
Outputs:
- focused_image: bfloat16 [2, 8, 512, 16384], P(None, ('scene', 'az'), None, 'bins'), parts along dimension 1
There are 2 independent parts, one for each index of `scene`. A program takes and returns all parts, laid end to end along the dimension named above; an argument that names none is the same for every part. Nothing has to cross between parts.
Inputs may be any that keep to these rules, and one draw needn't show every extreme that they name: band_start[b] - b lies between 0 and 64 for every range bin b.
All inputs are finite; a program needn't handle non-finite values.
Results may differ from a plain program's by a relative error of at most 0.02.
Values may be sent and summed in bfloat16 or wider, within the bound.
A program may use at most 128 MiB of HBM per device.

v0:
```python
import math
import jax
import jax.numpy as jnp
from jax import lax
from jax.sharding import PartitionSpec as P

OVLMAX = 128


def passed_along(value, axis, steps):
    count = lax.axis_size(axis)
    first, last = (max(0, -steps), min(count, count - steps))
    return lax.ppermute(value, axis, [(source, source + steps) for source in range(first, last)])


def phase_pair(row_count, col_count, length, direction):
    row_index = jnp.arange(row_count, dtype=jnp.int32)[:, None]
    col_index = jnp.arange(col_count, dtype=jnp.int32)[None, :]
    product = (row_index * col_index % length).astype(jnp.float32)
    phase_angle = product * (direction * 2.0 * math.pi / length)
    return (jnp.cos(phase_angle), jnp.sin(phase_angle))


def narrow_pair(operands):
    return (operands[0].astype(jnp.bfloat16), operands[1].astype(jnp.bfloat16))


def complex_product(form, left_pair, right_pair):
    left_real, left_imag = left_pair
    right_real, right_imag = right_pair
    real_part = jnp.einsum(
        form, left_real, right_real, preferred_element_type=jnp.float32
    ) - jnp.einsum(form, left_imag, right_imag, preferred_element_type=jnp.float32)
    imag_part = jnp.einsum(
        form, left_real, right_imag, preferred_element_type=jnp.float32
    ) + jnp.einsum(form, left_imag, right_real, preferred_element_type=jnp.float32)
    return (real_part, imag_part)


def complex_scale(operands, cosine, sine_part):
    real_part = operands[0] * cosine - operands[1] * sine_part
    imag_part = operands[0] * sine_part + operands[1] * cosine
    return (real_part, imag_part)


def compress_lines(echo_lines, range_phase):
    line_count, line_width = (echo_lines.shape[1], echo_lines.shape[2])
    radix_size = 128
    other_size = line_width // radix_size
    line_grid = echo_lines.reshape(2, line_count, radix_size, other_size)
    first_table = narrow_pair(phase_pair(radix_size, radix_size, radix_size, -1.0))
    partial_value = complex_product("ka,pan->pkn", first_table, (line_grid[0], line_grid[1]))
    partial_value = complex_scale(
        partial_value, *phase_pair(radix_size, other_size, line_width, -1.0)
    )
    second_table = narrow_pair(phase_pair(other_size, other_size, other_size, -1.0))
    spectrum = complex_product("pkn,nm->pkm", narrow_pair(partial_value), second_table)
    filter_angle = range_phase.reshape(other_size, radix_size).T
    filtered = narrow_pair(complex_scale(spectrum, jnp.cos(filter_angle), -jnp.sin(filter_angle)))
    back_table = narrow_pair(phase_pair(other_size, other_size, other_size, 1.0))
    partial_value = complex_product("pkm,mn->pkn", filtered, back_table)
    partial_value = complex_scale(
        partial_value, *phase_pair(radix_size, other_size, line_width, 1.0)
    )
    last_table = narrow_pair(phase_pair(radix_size, radix_size, radix_size, 1.0))
    result = complex_product("ak,pkn->pan", last_table, narrow_pair(partial_value))
    stacked = jnp.stack(result) * (1.0 / line_width)
    return stacked.reshape(2, line_count, line_width).astype(jnp.bfloat16)


def migrate(samples, range_rim, starts, weights):
    row_count, line_width = (samples.shape[1], samples.shape[2])
    blocks = line_width // 128
    extended = jnp.concatenate([samples, range_rim], axis=2)
    windows = jnp.concatenate(
        [
            extended[:, :, :line_width].reshape(2, row_count, blocks, 128),
            extended[:, :, 128:].reshape(2, row_count, blocks, 128),
        ],
        axis=3,
    )
    block_start = 128 * jnp.arange(blocks, dtype=jnp.int32)[:, None]
    offsets = starts.reshape(blocks, 128) - block_start
    position = jnp.arange(256, dtype=jnp.int32)[None, :, None]
    band_matrix = jnp.zeros((blocks, 256, 128), jnp.bfloat16)
    for tap_index in range(weights.shape[0]):
        tap_weight = weights[tap_index].reshape(blocks, 128)[:, None, :]
        band_matrix = band_matrix + jnp.where(
            position == (offsets + tap_index)[:, None, :], tap_weight, jnp.zeros((), jnp.bfloat16)
        )
    result = jnp.einsum("sprj,rjk->sprk", windows, band_matrix, preferred_element_type=jnp.float32)
    return result.reshape(2, row_count, line_width).astype(jnp.bfloat16)


def shards(raw_echoes, range_phase, band_start, band_weight, intersection_length, azimuth_rate):
    echo_lines = raw_echoes[:, 0]
    compressed = compress_lines(echo_lines, range_phase)
    empty_rim = jnp.zeros((2, compressed.shape[1], 128), jnp.bfloat16)
    outgoing = migrate(compressed, empty_rim, band_start, band_weight)
    turned = lax.all_to_all(outgoing, "bins", split_axis=2, concat_axis=1, tiled=True)
    head_lines = passed_along(turned[:, :OVLMAX], "az", -1)
    aperture = jnp.concatenate([turned, head_lines], axis=1)
    own_count = turned.shape[1]
    length = aperture.shape[1]
    pulses = jnp.arange(length, dtype=jnp.int32)[:, None]
    inside = (pulses < own_count) | (pulses - own_count < intersection_length[None, :])
    aperture = jnp.where(inside[None], aperture, jnp.zeros((), jnp.bfloat16))
    forward_table = narrow_pair(phase_pair(length, length, length, -1.0))
    spectrum = complex_product("fp,pr->fr", forward_table, (aperture[0], aperture[1]))
    doppler = jnp.arange(length, dtype=jnp.int32)
    signed = jnp.where(2 * doppler >= length, doppler - length, doppler).astype(jnp.float32)
    phase_angle = math.pi * azimuth_rate[None, :] * (signed * signed)[:, None] / length
    focused = narrow_pair(complex_scale(spectrum, jnp.cos(phase_angle), -jnp.sin(phase_angle)))
    inverse_table = narrow_pair(phase_pair(own_count, length, length, 1.0))
    image_pair = complex_product("qf,fr->qr", inverse_table, focused)
    stacked = jnp.stack(image_pair) * (1.0 / length)
    return stacked.astype(jnp.bfloat16)[:, None]


def solution(mesh):
    in_specs = (P(None, ("scene", "az"), "bins", None), P(), P(), P(), P("bins"), P("bins"))
    out_specs = P(None, ("scene", "az"), None, "bins")
    return jax.shard_map(shards, mesh=mesh, in_specs=in_specs, out_specs=out_specs, check_vma=False)
```

profile of v0, /device:TPU:1, one launch (start us, length us, event | category | flops | bytes accessed | tf_op | source)
XLA Modules:
  0.0 641.5 jit_solution(2054546862084710419)
XLA Ops:
  20.9 10.6 %fusion.42 = (bf16[128,128,128]{2,1,0:T(8,128)(2,1)S(1)}, bf16[128,128,128]{2,1,0:T(8,128)(2,1)S(1)}) fusion(f32[128,128]{1,0:T(8,128)S(1)} %get-tuple-element.37, f32[128,128]{1,0:T(8,128)S(1)} %get-tuple-element.38, f32[128,128,128]{2,0,1:T(8,128)} %fusion.105, f32[128,128,128]{2,0,1:T(8,128)} %fusion.97, f32[128,128,128]{2,0,1:T(8,128)} %fusion.99, ...), kind=kOutput, calls=%fused_computation.64 | convolution fusion | flops 558088192 | bytes 37879808 | tf_op jit(solution)/shard_map/ka,pan->pkn/dot_general | solution.py:31
  46.2 13.0 %add_convert_fusion.2 = (bf16[128,128,128]{2,1,0:T(8,128)(2,1)S(1)}, bf16[128,128,128]{2,1,0:T(8,128)(2,1)S(1)}) fusion(f32[128,128]{1,0:T(8,128)S(1)} %copy.36, f32[128,128]{1,0:T(8,128)S(1)} %copy.35, f32[128,128,128]{2,1,0:T(8,128)} %fusion.101, f32[128,128,128]{2,1,0:T(8,128)} %fusion.103, f32[128,128,128]{2,1,0:T(8,128)} %fusion.95, ...), kind=kOutput, calls=%fused_computation.45 | convolution fusion | flops 558088192 | bytes 37879808 | tf_op jit(solution)/shard_map/pkn,nm->pkm/dot_general | solution.py:34
  63.9 4.9 fusion.89
  73.8 12.9 %subtract_convert_fusion.1 = (bf16[128,128,128]{2,1,0:T(8,128)(2,1)}, bf16[128,128,128]{2,1,0:T(8,128)(2,1)S(1)}) fusion(f32[128,128]{1,0:T(8,128)S(1)} %get-tuple-element.39, f32[128,128]{1,0:T(8,128)S(1)} %get-tuple-element.40, f32[128,128,128]{2,1,0:T(8,128)} %fusion.89, f32[128,128,128]{2,1,0:T(8,128)} %fusion.91, f32[128,128,128]{2,1,0:T(8,128)} %fusion.83, ...), kind=kOutput, calls=%fused_computation.44 | convolution fusion | flops 558088192 | bytes 37879808 | tf_op jit(solution)/shard_map/pkm,mn->pkn/dot_general | solution.py:34
  86.7 4.9 fusion.79
  93.1 10.6 %subtract_bitcast_fusion.1 = (f32[1,128,128,128]{2,3,1,0:T(8,128)}, f32[128,128,128]{1,2,0:T(8,128)}) fusion(f32[128,128,128]{2,1,0:T(8,128)} %fusion.79, bf16[128,128,128]{2,1,0:T(8,128)(2,1)S(1)} %copy-done.1), kind=kOutput, calls=%fused_computation.78 | convolution fusion | flops 539213824 | bytes 29360128 | tf_op jit(solution)/shard_map/ak,pkn->pan/dot_general | solution.py:31
  103.7 7.5 %add_bitcast_fusion.1 = (f32[1,128,128,128]{2,3,1,0:T(8,128)}, f32[128,128,128]{1,2,0:T(8,128)}) fusion(f32[128,128,128]{2,1,0:T(8,128)S(1)} %fusion.77, bf16[128,128,128]{2,1,0:T(8,128)(2,1)S(1)} %get-tuple-element.16), kind=kOutput, calls=%fused_computation.76 | convolution fusion | flops 539213824 | bytes 29360128 | tf_op jit(solution)/shard_map/ak,pkn->pan/dot_general | solution.py:34
  111.2 9.4 %copy.41 = f32[128,128,128]{0,2,1:T(8,128)} copy(f32[128,128,128]{1,2,0:T(8,128)} %get-tuple-element.24) | data formatting | bytes 16777216 | tf_op jit(solution)/shard_map/sub | solution.py:31
  120.6 9.4 %copy.42 = f32[128,128,128]{0,2,1:T(8,128)} copy(f32[128,128,128]{1,2,0:T(8,128)} %get-tuple-element.26) | data formatting | bytes 16777216 | tf_op jit(solution)/shard_map/add | solution.py:34
  130.1 6.7 %fusion.1 = bf16[2,128,16384]{1,2,0:T(8,128)(2,1)S(1)} fusion(f32[1,128,16384]{1,2,0:T(8,128)} %bitcast.146, f32[1,128,16384]{1,2,0:T(8,128)} %bitcast.145), kind=kLoop, calls=%fused_computation.3 | loop fusion | flops 12582912 | bytes 25165824 | tf_op jit(solution)/shard_map/convert_element_type | solution.py:68
  140.4 13.6 %copy.43 = bf16[2,128,128,128]{2,3,1,0:T(8,128)(2,1)} copy(bf16[2,128,128,128]{1,3,2,0:T(8,128)(2,1)} %bitcast.147) | data formatting | bytes 16777216 | tf_op jit(solution)/shard_map/reshape | solution.py:78
  154.0 7.1 %fusion = bf16[2,128,128,128]{2,3,1,0:T(8,128)(2,1)S(1)} fusion(f32[1,128,128,128]{2,3,1,0:T(8,128)} %get-tuple-element.25, f32[1,128,128,128]{2,3,1,0:T(8,128)} %get-tuple-element.23), kind=kLoop, calls=%fused_computation.1 | loop fusion | flops 12582912 | bytes 25165824 | tf_op jit(solution)/shard_map/convert_element_type | solution.py:68
  162.2 6.5 %pad_maximum_fusion = bf16[2,128,128,256]{2,3,1,0:T(8,128)(2,1)} fusion(bf16[2,128,128,128]{2,3,1,0:T(8,128)(2,1)S(1)} %copy-done.2, bf16[2,128,128,128]{2,3,1,0:T(8,128)(2,1)S(1)} %fusion), kind=kLoop, calls=%fused_computation.4 | loop fusion | flops 33554432 | bytes 33554432 | tf_op jit(solution)/shard_map/concatenate | solution.py:75
  168.7 23.6 %copy.44 = bf16[2,128,128,256]{3,1,0,2:T(8,128)(2,1)} copy(bf16[2,128,128,256]{2,3,1,0:T(8,128)(2,1)} %pad_maximum_fusion) | data formatting | bytes 33554432 | tf_op jit(solution)/shard_map/concatenate | solution.py:75
  193.9 38.2 %fusion.232 = bf16[128,256,128,1]{1,2,3,0:T(8,128)(2,1)} fusion(s32[128,128]{1,0:T(8,128)S(1)} %get-tuple-element.34, s32[128,128]{1,0:T(8,128)S(1)} %get-tuple-element.30, s32[128,128]{1,0:T(8,128)S(1)} %get-tuple-element.31, s32[128,128]{1,0:T(8,128)S(1)} %get-tuple-element.32, s32[128,128]{1,0:T(8,128)S(1)} %get-tuple-element.33, ...), kind=kLoop, calls=%fused_computation.32.clone.clone.clone.clone.1 | loop fusion | flops 134217728 | bytes 9175040 | tf_op jit(solution)/shard_map/sprj,rjk->sprk/dot_general | solution.py:91
  232.1 13.1 %convert_bitcast_fusion = bf16[2,128,128,128]{1,3,0,2:T(8,128)(2,1)} fusion(bf16[2,128,128,256]{3,1,0,2:T(8,128)(2,1)} %copy.44, bf16[128,256,128,1]{1,2,3,0:T(8,128)(2,1)} %fusion.232), kind=kOutput, calls=%fused_computation.42 | convolution fusion | flops 2151677952 | bytes 33554432 | tf_op jit(solution)/shard_map/sprj,rjk->sprk/dot_general | solution.py:91
  245.2 10.5 %copy.45 = bf16[2,128,128,128]{1,3,2,0:T(8,128)(2,1)} copy(bf16[2,128,128,128]{1,3,0,2:T(8,128)(2,1)} %convert_bitcast_fusion) | data formatting | bytes 16777216 | tf_op jit(solution)/shard_map/convert_element_type | solution.py:92
  255.7 15.6 %copy.46 = bf16[2,128,16384]{1,0,2:T(2,128)(2,1)S(1)} copy(bf16[2,128,16384]{1,2,0:T(8,128)(2,1)} %bitcast.148) | data formatting | bytes 16777216 | tf_op jit(solution)/shard_map/convert_element_type | solution.py:92
  271.3 187.4 %all_to_all.18 = bf16[2,128,16384]{1,0,2:T(2,128)(2,1)S(1)} all-to-all(bf16[2,128,16384]{1,0,2:T(2,128)(2,1)S(1)} %copy.46), channel_id=1, replica_groups=mesh['scene'=2,'bins'=4,'az'=4] {'bins'}, dimensions={2} | all-to-all | bytes 16777216 | tf_op jit(solution)/shard_map/all_to_all | solution.py:100
  458.7 10.5 %copy.47 = bf16[2,128,16384]{1,2,0:T(8,128)(2,1)} copy(bf16[2,128,16384]{1,0,2:T(2,128)(2,1)S(1)} %all_to_all.18) | data formatting | bytes 16777216 | tf_op jit(solution)/shard_map/all_to_all | solution.py:100
  469.3 12.1 %copy.48 = bf16[2,4,128,4096]{3,2,1,0:T(8,128)(2,1)} copy(bf16[2,4,128,4096]{2,3,1,0:T(8,128)(2,1)} %bitcast.149) | data formatting | bytes 16777216 | tf_op jit(solution)/shard_map/all_to_all | solution.py:100
  486.8 6.5 %cosine_convert_fusion.2.clone.5 = bf16[640,640]{1,0:T(8,128)(2,1)S(1)} fusion(), kind=kLoop, calls=%fused_computation.85.clone.clone.clone.clone.2 | loop fusion | flops 4096000 | bytes 819200 | tf_op jit(solution)/shard_map/convert_element_type | solution.py:25
  495.7 15.8 %collective-permute-done = bf16[2,128,4096]{2,1,0:T(8,128)(2,1)S(1)} collective-permute-done((bf16[2,128,4096]{2,1,0:T(8,128)(2,1)S(1)}, bf16[2,128,4096]{2,1,0:T(8,128)(2,1)S(1)}, u32[]{:S(2)}, u32[]{:S(2)}) %collective-permute-start) | collective-permute-done | bytes 2097184 | tf_op jit(solution)/shard_map/ppermute | solution.py:13
  511.6 7.9 %maximum_select_fusion = bf16[2,640,4096]{2,1,0:T(8,128)(2,1)S(1)} fusion(bf16[2,128,4096]{2,1,0:T(8,128)(2,1)S(1)} %collective-permute-done, bf16[2,512,4096]{2,1,0:T(8,128)(2,1)} %bitcast.140, pred[640,4096]{1,0:T(8,128)(4,1)S(1)} %compare_or_fusion), kind=kLoop, calls=%fused_computation.23 | loop fusion | flops 26214400 | bytes 23592960 | tf_op jit(solution)/shard_map/jit(_where)/select_n | solution.py:107
  519.5 12.6 %fusion.40 = f32[640,4096]{1,0:T(8,128)} fusion(bf16[2,640,4096]{2,1,0:T(8,128)(2,1)S(1)} %maximum_select_fusion), kind=kOutput, calls=%fused_computation.62 | convolution fusion | flops 3359539200 | bytes 15728640 | tf_op jit(solution)/shard_map/fp,pr->fr/dot_general | solution.py:33
  532.1 12.9 %fusion.39 = f32[640,4096]{1,0:T(8,128)} fusion(bf16[2,640,4096]{2,1,0:T(8,128)(2,1)S(1)} %maximum_select_fusion), kind=kOutput, calls=%fused_computation.61 | convolution fusion | flops 3359539200 | bytes 15728640 | tf_op jit(solution)/shard_map/fp,pr->fr/dot_general | solution.py:36
  545.0 12.9 %convolution_subtract_fusion = f32[640,4096]{1,0:T(8,128)S(1)} fusion(f32[640,4096]{1,0:T(8,128)} %fusion.40, bf16[2,640,4096]{2,1,0:T(8,128)(2,1)S(1)} %maximum_select_fusion), kind=kOutput, calls=%fused_computation.58 | convolution fusion | flops 3362160640 | bytes 26214400 | tf_op jit(solution)/shard_map/fp,pr->fr/dot_general | solution.py:31
  557.9 46.4 %subtract_convert_fusion = (bf16[640,4096]{1,0:T(8,128)(2,1)S(1)}, bf16[640,4096]{1,0:T(8,128)(2,1)}) fusion(f32[640,4096]{1,0:T(8,128)S(1)} %convolution_subtract_fusion, f32[640]{0:T(1024)S(1)} %fusion.111, f32[4096]{0:T(1024)S(1)} %broadcast_multiply_fusion, f32[640,4096]{1,0:T(8,128)} %fusion.39, bf16[2,640,4096]{2,1,0:T(8,128)(2,1)S(1)} %maximum_select_fusion, ...), kind=kOutput, calls=%fused_computation.25 | convolution fusion | flops 3386900480 | bytes 37539840 | tf_op jit(solution)/shard_map/fp,pr->fr/dot_general | solution.py:34
  604.4 8.0 %fusion.63 = f32[512,4096]{1,0:T(8,128)S(1)} fusion(bf16[640,4096]{1,0:T(8,128)(2,1)S(1)} %get-tuple-element.21), kind=kOutput, calls=%fused_computation.99 | convolution fusion | flops 2687631360 | bytes 13631488 | tf_op jit(solution)/shard_map/qf,fr->qr/dot_general | solution.py:31
  612.4 8.4 %fusion.62 = f32[512,4096]{1,0:T(8,128)S(1)} fusion(bf16[640,4096]{1,0:T(8,128)(2,1)S(1)} %bitcast.159), kind=kOutput, calls=%fused_computation.98 | convolution fusion | flops 2687631360 | bytes 13631488 | tf_op jit(solution)/shard_map/qf,fr->qr/dot_general | solution.py:34
  620.9 8.1 %subtract_bitcast_fusion = f32[1,1,512,4096]{3,2,1,0:T(8,128)S(1)} fusion(f32[512,4096]{1,0:T(8,128)S(1)} %fusion.63, bf16[640,4096]{1,0:T(8,128)(2,1)S(1)} %bitcast.159), kind=kOutput, calls=%fused_computation.41 | convolution fusion | flops 2689728512 | bytes 22020096 | tf_op jit(solution)/shard_map/qf,fr->qr/dot_general | solution.py:33
  629.0 8.3 %add_bitcast_fusion = f32[1,1,512,4096]{3,2,1,0:T(8,128)S(1)} fusion(f32[512,4096]{1,0:T(8,128)S(1)} %fusion.62, bf16[640,4096]{1,0:T(8,128)(2,1)S(1)} %copy-done.9), kind=kOutput, calls=%fused_computation.40 | convolution fusion | flops 2689728512 | bytes 22020096 | tf_op jit(solution)/shard_map/qf,fr->qr/dot_general | solution.py:36
  (55 shorter events, 64.9 us)
Async XLA Ops:
  31.5 9.6 %copy-start = (bf16[128,128,128]{2,1,0:T(8,128)(2,1)}, bf16[128,128,128]{2,1,0:T(8,128)(2,1)S(1)}, u32[]{:S(2)}) copy-start(bf16[128,128,128]{2,1,0:T(8,128)(2,1)S(1)} %get-tuple-element.20) | copy-start | bytes 12582916
  41.1 4.7 copy-start.4
  86.7 4.9 copy-start.1
  154.0 8.2 %copy-start.2 = (bf16[2,128,128,128]{2,3,1,0:T(8,128)(2,1)S(1)}, bf16[2,128,128,128]{2,3,1,0:T(8,128)(2,1)}, u32[]{:S(2)}) copy-start(bf16[2,128,128,128]{2,3,1,0:T(8,128)(2,1)} %copy.43) | copy-start | bytes 25165828
  168.7 23.7 %copy-start.5 = (s32[16384]{0:T(1024)S(1)}, s32[16384]{0:T(1024)}, u32[]{:S(2)}) copy-start(s32[16384]{0:T(1024)} %param.8) | copy-start | bytes 196612
  168.7 23.8 %copy-start.3 = (bf16[8,16384]{1,0:T(8,128)(2,1)S(1)}, bf16[8,16384]{1,0:T(8,128)(2,1)}, u32[]{:S(2)}) copy-start(bf16[8,16384]{1,0:T(8,128)(2,1)} %param.9) | copy-start | bytes 786436
  469.3 24.1 %copy-start.7 = (f32[4096]{0:T(1024)S(1)}, f32[4096]{0:T(1024)}, u32[]{:S(2)}) copy-start(f32[4096]{0:T(1024)} %param.11) | copy-start | bytes 49156
  469.3 24.1 %copy-start.6 = (s32[4096]{0:T(1024)S(1)}, s32[4096]{0:T(1024)}, u32[]{:S(2)}) copy-start(s32[4096]{0:T(1024)} %param.10) | copy-start | bytes 49156
  483.1 28.5 %collective-permute-start = (bf16[2,128,4096]{2,1,0:T(8,128)(2,1)S(1)}, bf16[2,128,4096]{2,1,0:T(8,128)(2,1)S(1)}, u32[]{:S(2)}, u32[]{:S(2)}) collective-permute-start(bf16[2,128,4096]{2,1,0:T(8,128)(2,1)S(1)} %slice.58), channel_id=1, source_target_pairs={{1,0},{2,1},{3,2},{5,4},{6,5},{7,6},{9,8},{10,9},{11,10},{13,12},{... | collective-permute-start | bytes 6291464 | tf_op jit(solution)/shard_map/ppermute | solution.py:13
  604.3 8.1 %copy-start.8 = (bf16[640,4096]{1,0:T(8,128)(2,1)}, bf16[640,4096]{1,0:T(8,128)(2,1)S(1)}, u32[]{:S(2)}) copy-start(bf16[640,4096]{1,0:T(8,128)(2,1)S(1)} %get-tuple-element.21) | copy-start | bytes 15728644
  604.3 8.1 %slice-start = ((s8[5242880]{0:T(1024)(128)(4,1)}), s8[4194304]{0:T(1024)(128)(4,1)S(1)}, s32[]{:S(2)}) async-start(s8[5242880]{0:T(1024)(128)(4,1)} %bitcast.158), calls=%async_computation.1 | async-start | bytes 8388608
  604.4 8.1 %slice-start.1 = ((s8[5242880]{0:T(1024)(128)(4,1)}), s8[1048576]{0:T(1024)(128)(4,1)S(1)}, s32[]{:S(2)}) async-start(s8[5242880]{0:T(1024)(128)(4,1)} %bitcast.158), calls=%async_computation.2 | async-start | bytes 2097152
  620.9 8.1 %copy-start.9 = (bf16[640,4096]{1,0:T(8,128)(2,1)S(1)}, bf16[640,4096]{1,0:T(8,128)(2,1)}, u32[]{:S(2)}) copy-start(bf16[640,4096]{1,0:T(8,128)(2,1)} %copy-done.8) | copy-start | bytes 15728644
where the time goes:
time: 649 us; the launch traced here: 642 us
  matrix products  234 us (36%)
  blocking collectives  187 us (29%)
  local copies, waits for them, and re-layouts  119 us (18%)
  other arithmetic  80.3 us (12%)
  waiting for transfers between devices  15.8 us (2%)
    all_to_all x1, blocking collectives, shards(): lax.all_to_all(outgoing, 'bins', split_axis=2, concat_axis=1, tiled=True)  187 us
    dot_general x6, matrix products, complex_product(): jnp.einsum(form, left_real, right_imag, preferred_element_type=jnp.float32)  93.1 us
    dot_general x6, matrix products, complex_product(): jnp.einsum(form, left_real, right_real, preferred_element_type=jnp.float32)  51.5 us
    dot_general x6, matrix products, complex_product(): jnp.einsum(form, left_imag, right_imag, preferred_element_type=jnp.float32)  39.7 us
    dot_general x1, other arithmetic, migrate(): jnp.einsum('sprj,rjk->sprk', windows, band_matrix, preferred_element_type...  38.2 us
    dot_general x6, matrix products, complex_product(): jnp.einsum(form, left_imag, right_real, preferred_element_type=jnp.float32)  37.1 us
    convert_element_type x2, local copies, waits for them, and re-layouts, migrate(): return result.reshape(2, row_count, line_width).astype(jnp.bfloat16)  26.1 us
    concatenate x1, local copies, waits for them, and re-layouts, migrate(): jnp.concatenate([extended[:, :, :line_width].reshape(2, row_count, blocks...  23.6 us
  transfers between devices with their start and end apart: 1, of which 1 were waited for; matrix products, arithmetic and copies ran while one was open for 1% of the time, Pallas kernels for 0%

commit v1 on v0

--- a/solution.py
+++ b/solution.py
@@ -97,7 +97,10 @@
     compressed = compress_lines(echo_lines, range_phase)
     empty_rim = jnp.zeros((2, compressed.shape[1], 128), jnp.bfloat16)
     outgoing = migrate(compressed, empty_rim, band_start, band_weight)
-    turned = lax.all_to_all(outgoing, "bins", split_axis=2, concat_axis=1, tiled=True)
+    turned = jnp.concatenate(
+        lax.all_to_all(jnp.stack(jnp.split(outgoing, lax.axis_size("bins"), axis=2)), "bins", 0, 0),
+        axis=1,
+    )
     head_lines = passed_along(turned[:, :OVLMAX], "az", -1)
     aperture = jnp.concatenate([turned, head_lines], axis=1)
     own_count = turned.shape[1]

time: 649 us -> 628 us (0.968)
  local copies, waits for them, and re-layouts: 119 us -> 96.6 us
    all_to_all x2 -> x0, local copies, waits for them, and re-layouts: 22.6 us -> none  [shards(): lax.all_to_all(outgoing, 'bins', split_axis=2, concat_axis=1, tiled=True)]
    convert_element_type x2 -> x1, local copies, waits for them, and re-layouts: 26.1 us -> 10.5 us  [migrate(): return result.reshape(2, row_count, line_width).astype(jnp.bfloat16)]
    reshape x0 -> x1, local copies, waits for them, and re-layouts: none -> 12 us  [shards(): jnp.concatenate(lax.all_to_all(jnp.stack(jnp.split(outgoing, lax.axis_siz...]
where the time goes in v1:
time: 628 us; the launch traced here: 620 us
  matrix products  235 us (37%)
  blocking collectives  188 us (30%)
  local copies, waits for them, and re-layouts  96.6 us (15%)
  other arithmetic  81.5 us (13%)
  waiting for transfers between devices  15.8 us (3%)
    all_to_all x1, blocking collectives, shards(): lax.all_to_all(jnp.stack(jnp.split(outgoing, lax.axis_size('bins'), axis=...  188 us
    dot_general x6, matrix products, complex_product(): jnp.einsum(form, left_real, right_imag, preferred_element_type=jnp.float32)  93.1 us
    dot_general x6, matrix products, complex_product(): jnp.einsum(form, left_real, right_real, preferred_element_type=jnp.float32)  51.5 us
    dot_general x6, matrix products, complex_product(): jnp.einsum(form, left_imag, right_imag, preferred_element_type=jnp.float32)  39.7 us
    dot_general x1, other arithmetic, migrate(): jnp.einsum('sprj,rjk->sprk', windows, band_matrix, preferred_element_type...  38.2 us
    dot_general x6, matrix products, complex_product(): jnp.einsum(form, left_imag, right_real, preferred_element_type=jnp.float32)  37.1 us
    concatenate x1, local copies, waits for them, and re-layouts, migrate(): jnp.concatenate([extended[:, :, :line_width].reshape(2, row_count, blocks...  23.7 us
    ppermute x1, waiting for transfers between devices, passed_along(): lax.ppermute(value, axis, [(source, source + steps) for source in range(f...  15.8 us
  transfers between devices with their start and end apart: 1, of which 1 were waited for; matrix products, arithmetic and copies ran while one was open for 1% of the time, Pallas kernels for 0%

profile of v1, /device:TPU:1, one launch (start us, length us, event | category | flops | bytes accessed | tf_op | source)
XLA Modules:
  0.0 620.3 jit_solution(1054975798849662732)
XLA Ops:
  5.1 4.9 fusion.105
  20.9 10.6 %fusion.42 = (bf16[128,128,128]{2,1,0:T(8,128)(2,1)S(1)}, bf16[128,128,128]{2,1,0:T(8,128)(2,1)S(1)}) fusion(f32[128,128]{1,0:T(8,128)S(1)} %get-tuple-element.41, f32[128,128]{1,0:T(8,128)S(1)} %get-tuple-element.42, f32[128,128,128]{2,0,1:T(8,128)} %fusion.105, f32[128,128,128]{2,0,1:T(8,128)} %fusion.97, f32[128,128,128]{2,0,1:T(8,128)} %fusion.99, ...), kind=kOutput, calls=%fused_computation.65 | convolution fusion | flops 558088192 | bytes 37879808 | tf_op jit(solution)/shard_map/ka,pan->pkn/dot_general | solution.py:31
  31.5 4.9 fusion.101
  46.2 13.0 %add_convert_fusion.2 = (bf16[128,128,128]{2,1,0:T(8,128)(2,1)S(1)}, bf16[128,128,128]{2,1,0:T(8,128)(2,1)S(1)}) fusion(f32[128,128]{1,0:T(8,128)S(1)} %copy.27, f32[128,128]{1,0:T(8,128)S(1)} %copy.26, f32[128,128,128]{2,1,0:T(8,128)} %fusion.101, f32[128,128,128]{2,1,0:T(8,128)} %fusion.103, f32[128,128,128]{2,1,0:T(8,128)} %fusion.95, ...), kind=kOutput, calls=%fused_computation.46 | convolution fusion | flops 558088192 | bytes 37879808 | tf_op jit(solution)/shard_map/pkn,nm->pkm/dot_general | solution.py:34
  63.9 4.9 fusion.89
  73.8 12.9 %subtract_convert_fusion.1 = (bf16[128,128,128]{2,1,0:T(8,128)(2,1)}, bf16[128,128,128]{2,1,0:T(8,128)(2,1)S(1)}) fusion(f32[128,128]{1,0:T(8,128)S(1)} %get-tuple-element.43, f32[128,128]{1,0:T(8,128)S(1)} %get-tuple-element.44, f32[128,128,128]{2,1,0:T(8,128)} %fusion.89, f32[128,128,128]{2,1,0:T(8,128)} %fusion.91, f32[128,128,128]{2,1,0:T(8,128)} %fusion.83, ...), kind=kOutput, calls=%fused_computation.45 | convolution fusion | flops 558088192 | bytes 37879808 | tf_op jit(solution)/shard_map/pkm,mn->pkn/dot_general | solution.py:34
  86.7 4.9 fusion.79
  93.1 10.6 %subtract_bitcast_fusion.1 = (f32[1,128,128,128]{2,3,1,0:T(8,128)}, f32[128,128,128]{1,2,0:T(8,128)}) fusion(f32[128,128,128]{2,1,0:T(8,128)} %fusion.79, bf16[128,128,128]{2,1,0:T(8,128)(2,1)S(1)} %copy-done.1), kind=kOutput, calls=%fused_computation.79 | convolution fusion | flops 539213824 | bytes 29360128 | tf_op jit(solution)/shard_map/ak,pkn->pan/dot_general | solution.py:31
  103.8 7.5 %add_bitcast_fusion.1 = (f32[1,128,128,128]{2,3,1,0:T(8,128)}, f32[128,128,128]{1,2,0:T(8,128)}) fusion(f32[128,128,128]{2,1,0:T(8,128)S(1)} %fusion.77, bf16[128,128,128]{2,1,0:T(8,128)(2,1)S(1)} %get-tuple-element.16), kind=kOutput, calls=%fused_computation.77 | convolution fusion | flops 539213824 | bytes 29360128 | tf_op jit(solution)/shard_map/ak,pkn->pan/dot_general | solution.py:34
  111.3 9.4 %copy.32 = f32[128,128,128]{0,2,1:T(8,128)} copy(f32[128,128,128]{1,2,0:T(8,128)} %get-tuple-element.24) | data formatting | bytes 16777216 | tf_op jit(solution)/shard_map/sub | solution.py:31
  120.7 9.4 %copy.33 = f32[128,128,128]{0,2,1:T(8,128)} copy(f32[128,128,128]{1,2,0:T(8,128)} %get-tuple-element.26) | data formatting | bytes 16777216 | tf_op jit(solution)/shard_map/add | solution.py:34
  130.1 6.7 %fusion.1 = bf16[2,128,16384]{1,2,0:T(8,128)(2,1)S(1)} fusion(f32[1,128,16384]{1,2,0:T(8,128)} %bitcast.152, f32[1,128,16384]{1,2,0:T(8,128)} %bitcast.151), kind=kLoop, calls=%fused_computation.3 | loop fusion | flops 12582912 | bytes 25165824 | tf_op jit(solution)/shard_map/convert_element_type | solution.py:68
  140.4 13.5 %copy.34 = bf16[2,128,128,128]{2,3,1,0:T(8,128)(2,1)} copy(bf16[2,128,128,128]{1,3,2,0:T(8,128)(2,1)} %bitcast.154) | data formatting | bytes 16777216 | tf_op jit(solution)/shard_map/reshape | solution.py:78
  153.9 7.1 %fusion = bf16[2,128,128,128]{2,3,1,0:T(8,128)(2,1)S(1)} fusion(f32[1,128,128,128]{2,3,1,0:T(8,128)} %get-tuple-element.25, f32[1,128,128,128]{2,3,1,0:T(8,128)} %get-tuple-element.23), kind=kLoop, calls=%fused_computation.1 | loop fusion | flops 12582912 | bytes 25165824 | tf_op jit(solution)/shard_map/convert_element_type | solution.py:68
  162.2 6.5 %pad_maximum_fusion = bf16[2,128,128,256]{2,3,1,0:T(8,128)(2,1)} fusion(bf16[2,128,128,128]{2,3,1,0:T(8,128)(2,1)S(1)} %copy-done.2, bf16[2,128,128,128]{2,3,1,0:T(8,128)(2,1)S(1)} %fusion), kind=kLoop, calls=%fused_computation.4 | loop fusion | flops 33554432 | bytes 33554432 | tf_op jit(solution)/shard_map/concatenate | solution.py:75
  168.7 23.7 %copy.35 = bf16[2,128,128,256]{3,1,0,2:T(8,128)(2,1)} copy(bf16[2,128,128,256]{2,3,1,0:T(8,128)(2,1)} %pad_maximum_fusion) | data formatting | bytes 33554432 | tf_op jit(solution)/shard_map/concatenate | solution.py:75
  193.9 38.2 %fusion.232 = bf16[128,256,128,1]{1,2,3,0:T(8,128)(2,1)} fusion(s32[128,128]{1,0:T(8,128)S(1)} %get-tuple-element.38, s32[128,128]{1,0:T(8,128)S(1)} %get-tuple-element.34, s32[128,128]{1,0:T(8,128)S(1)} %get-tuple-element.35, s32[128,128]{1,0:T(8,128)S(1)} %get-tuple-element.36, s32[128,128]{1,0:T(8,128)S(1)} %get-tuple-element.37, ...), kind=kLoop, calls=%fused_computation.32.clone.clone.clone.clone.1 | loop fusion | flops 134217728 | bytes 9175040 | tf_op jit(solution)/shard_map/sprj,rjk->sprk/dot_general | solution.py:91
  232.1 13.1 %convert_bitcast_fusion = bf16[2,128,128,128]{1,3,0,2:T(8,128)(2,1)} fusion(bf16[2,128,128,256]{3,1,0,2:T(8,128)(2,1)} %copy.35, bf16[128,256,128,1]{1,2,3,0:T(8,128)(2,1)} %fusion.232), kind=kOutput, calls=%fused_computation.43 | convolution fusion | flops 2151677952 | bytes 33554432 | tf_op jit(solution)/shard_map/sprj,rjk->sprk/dot_general | solution.py:91
  245.2 10.5 %copy.36 = bf16[2,128,128,128]{1,3,2,0:T(8,128)(2,1)} copy(bf16[2,128,128,128]{1,3,0,2:T(8,128)(2,1)} %convert_bitcast_fusion) | data formatting | bytes 16777216 | tf_op jit(solution)/shard_map/convert_element_type | solution.py:92
  260.5 187.5 %all_to_all.5 = bf16[4,2,128,4096]{2,3,1,0:T(8,128)(2,1)} all-to-all(bf16[4,2,128,4096]{2,3,1,0:T(8,128)(2,1)S(1)} %pad_maximum_fusion.1), channel_id=1, replica_groups=mesh['scene'=2,'bins'=4,'az'=4] {'bins'}, dimensions={0} | all-to-all | bytes 16777216 | tf_op jit(solution)/shard_map/all_to_all | solution.py:101
  448.1 12.0 %copy.37 = bf16[2,4,128,4096]{3,2,1,0:T(8,128)(2,1)} copy(bf16[2,4,128,4096]{2,3,0,1:T(8,128)(2,1)} %bitcast.155) | data formatting | bytes 16777216 | tf_op jit(solution)/shard_map/reshape | solution.py:100
  465.5 6.5 %cosine_convert_fusion.2.clone.5 = bf16[640,640]{1,0:T(8,128)(2,1)S(1)} fusion(), kind=kLoop, calls=%fused_computation.90.clone.clone.clone.clone.2 | loop fusion | flops 4096000 | bytes 819200 | tf_op jit(solution)/shard_map/convert_element_type | solution.py:25
  474.4 15.8 %collective-permute-done = bf16[2,128,4096]{2,1,0:T(8,128)(2,1)S(1)} collective-permute-done((bf16[2,128,4096]{2,1,0:T(8,128)(2,1)S(1)}, bf16[2,128,4096]{2,1,0:T(8,128)(2,1)S(1)}, u32[]{:S(2)}, u32[]{:S(2)}) %collective-permute-start) | collective-permute-done | bytes 2097184 | tf_op jit(solution)/shard_map/ppermute | solution.py:13
  490.3 7.9 %maximum_select_fusion = bf16[2,640,4096]{2,1,0:T(8,128)(2,1)S(1)} fusion(bf16[2,128,4096]{2,1,0:T(8,128)(2,1)S(1)} %collective-permute-done, bf16[2,512,4096]{2,1,0:T(8,128)(2,1)} %bitcast.146, pred[640,4096]{1,0:T(8,128)(4,1)S(1)} %compare_or_fusion), kind=kLoop, calls=%fused_computation.23 | loop fusion | flops 26214400 | bytes 23592960 | tf_op jit(solution)/shard_map/jit(_where)/select_n | solution.py:110
  498.2 12.6 %fusion.40 = f32[640,4096]{1,0:T(8,128)} fusion(bf16[2,640,4096]{2,1,0:T(8,128)(2,1)S(1)} %maximum_select_fusion), kind=kOutput, calls=%fused_computation.63 | convolution fusion | flops 3359539200 | bytes 15728640 | tf_op jit(solution)/shard_map/fp,pr->fr/dot_general | solution.py:33
  510.8 12.9 %fusion.39 = f32[640,4096]{1,0:T(8,128)} fusion(bf16[2,640,4096]{2,1,0:T(8,128)(2,1)S(1)} %maximum_select_fusion), kind=kOutput, calls=%fused_computation.62 | convolution fusion | flops 3359539200 | bytes 15728640 | tf_op jit(solution)/shard_map/fp,pr->fr/dot_general | solution.py:36
  523.8 12.9 %convolution_subtract_fusion = f32[640,4096]{1,0:T(8,128)S(1)} fusion(f32[640,4096]{1,0:T(8,128)} %fusion.40, bf16[2,640,4096]{2,1,0:T(8,128)(2,1)S(1)} %maximum_select_fusion), kind=kOutput, calls=%fused_computation.59 | convolution fusion | flops 3362160640 | bytes 26214400 | tf_op jit(solution)/shard_map/fp,pr->fr/dot_general | solution.py:31
  536.6 46.4 %subtract_convert_fusion = (bf16[640,4096]{1,0:T(8,128)(2,1)S(1)}, bf16[640,4096]{1,0:T(8,128)(2,1)}) fusion(f32[640,4096]{1,0:T(8,128)S(1)} %convolution_subtract_fusion, f32[640]{0:T(1024)S(1)} %fusion.111, f32[4096]{0:T(1024)S(1)} %broadcast_multiply_fusion, f32[640,4096]{1,0:T(8,128)} %fusion.39, bf16[2,640,4096]{2,1,0:T(8,128)(2,1)S(1)} %maximum_select_fusion, ...), kind=kOutput, calls=%fused_computation.25 | convolution fusion | flops 3386900480 | bytes 37539840 | tf_op jit(solution)/shard_map/fp,pr->fr/dot_general | solution.py:34
  583.1 8.0 %fusion.63 = f32[512,4096]{1,0:T(8,128)S(1)} fusion(bf16[640,4096]{1,0:T(8,128)(2,1)S(1)} %get-tuple-element.21), kind=kOutput, calls=%fused_computation.104 | convolution fusion | flops 2687631360 | bytes 13631488 | tf_op jit(solution)/shard_map/qf,fr->qr/dot_general | solution.py:31
  591.2 8.4 %fusion.62 = f32[512,4096]{1,0:T(8,128)S(1)} fusion(bf16[640,4096]{1,0:T(8,128)(2,1)S(1)} %bitcast.165), kind=kOutput, calls=%fused_computation.103 | convolution fusion | flops 2687631360 | bytes 13631488 | tf_op jit(solution)/shard_map/qf,fr->qr/dot_general | solution.py:34
  599.6 8.1 %subtract_bitcast_fusion = f32[1,1,512,4096]{3,2,1,0:T(8,128)S(1)} fusion(f32[512,4096]{1,0:T(8,128)S(1)} %fusion.63, bf16[640,4096]{1,0:T(8,128)(2,1)S(1)} %bitcast.165), kind=kOutput, calls=%fused_computation.42 | convolution fusion | flops 2689728512 | bytes 22020096 | tf_op jit(solution)/shard_map/qf,fr->qr/dot_general | solution.py:33
  607.7 8.3 %add_bitcast_fusion = f32[1,1,512,4096]{3,2,1,0:T(8,128)S(1)} fusion(f32[512,4096]{1,0:T(8,128)S(1)} %fusion.62, bf16[640,4096]{1,0:T(8,128)(2,1)S(1)} %copy-done.9), kind=kOutput, calls=%fused_computation.41 | convolution fusion | flops 2689728512 | bytes 22020096 | tf_op jit(solution)/shard_map/qf,fr->qr/dot_general | solution.py:36
  (55 shorter events, 60.1 us)
Async XLA Ops:
  31.5 9.6 %copy-start = (bf16[128,128,128]{2,1,0:T(8,128)(2,1)}, bf16[128,128,128]{2,1,0:T(8,128)(2,1)S(1)}, u32[]{:S(2)}) copy-start(bf16[128,128,128]{2,1,0:T(8,128)(2,1)S(1)} %get-tuple-element.20) | copy-start | bytes 12582916
  41.1 4.7 copy-start.4
  86.7 4.9 copy-start.1
  153.9 8.2 %copy-start.2 = (bf16[2,128,128,128]{2,3,1,0:T(8,128)(2,1)S(1)}, bf16[2,128,128,128]{2,3,1,0:T(8,128)(2,1)}, u32[]{:S(2)}) copy-start(bf16[2,128,128,128]{2,3,1,0:T(8,128)(2,1)} %copy.34) | copy-start | bytes 25165828
  168.7 23.7 %copy-start.5 = (s32[16384]{0:T(1024)S(1)}, s32[16384]{0:T(1024)}, u32[]{:S(2)}) copy-start(s32[16384]{0:T(1024)} %param.8) | copy-start | bytes 196612
  168.7 23.8 %copy-start.3 = (bf16[8,16384]{1,0:T(8,128)(2,1)S(1)}, bf16[8,16384]{1,0:T(8,128)(2,1)}, u32[]{:S(2)}) copy-start(bf16[8,16384]{1,0:T(8,128)(2,1)} %param.9) | copy-start | bytes 786436
  448.1 24.0 %copy-start.7 = (f32[4096]{0:T(1024)S(1)}, f32[4096]{0:T(1024)}, u32[]{:S(2)}) copy-start(f32[4096]{0:T(1024)} %param.11) | copy-start | bytes 49156
  448.1 24.0 %copy-start.6 = (s32[4096]{0:T(1024)S(1)}, s32[4096]{0:T(1024)}, u32[]{:S(2)}) copy-start(s32[4096]{0:T(1024)} %param.10) | copy-start | bytes 49156
  461.8 28.5 %collective-permute-start = (bf16[2,128,4096]{2,1,0:T(8,128)(2,1)S(1)}, bf16[2,128,4096]{2,1,0:T(8,128)(2,1)S(1)}, u32[]{:S(2)}, u32[]{:S(2)}) collective-permute-start(bf16[2,128,4096]{2,1,0:T(8,128)(2,1)S(1)} %slice.58), channel_id=1, source_target_pairs={{1,0},{2,1},{3,2},{5,4},{6,5},{7,6},{9,8},{10,9},{11,10},{13,12},{... | collective-permute-start | bytes 6291464 | tf_op jit(solution)/shard_map/ppermute | solution.py:13
  583.1 8.1 %copy-start.8 = (bf16[640,4096]{1,0:T(8,128)(2,1)}, bf16[640,4096]{1,0:T(8,128)(2,1)S(1)}, u32[]{:S(2)}) copy-start(bf16[640,4096]{1,0:T(8,128)(2,1)S(1)} %get-tuple-element.21) | copy-start | bytes 15728644
  583.1 8.1 %slice-start = ((s8[5242880]{0:T(1024)(128)(4,1)}), s8[4194304]{0:T(1024)(128)(4,1)S(1)}, s32[]{:S(2)}) async-start(s8[5242880]{0:T(1024)(128)(4,1)} %bitcast.164), calls=%async_computation.1 | async-start | bytes 8388608
  583.1 8.1 %slice-start.1 = ((s8[5242880]{0:T(1024)(128)(4,1)}), s8[1048576]{0:T(1024)(128)(4,1)S(1)}, s32[]{:S(2)}) async-start(s8[5242880]{0:T(1024)(128)(4,1)} %bitcast.164), calls=%async_computation.2 | async-start | bytes 2097152
  599.6 8.1 %copy-start.9 = (bf16[640,4096]{1,0:T(8,128)(2,1)S(1)}, bf16[640,4096]{1,0:T(8,128)(2,1)}, u32[]{:S(2)}) copy-start(bf16[640,4096]{1,0:T(8,128)(2,1)} %copy-done.8) | copy-start | bytes 15728644
